TPU v7x, 768 devices: a whole 4x8x12 slice. The times are simulated.
768 devices in a mesh: row: 24 (over z, core), col: 32 (over x, y).
Axes of the slice: x: 4, y: 8, z: 12, core: 2. Of those that a mesh axis runs over, the one named last changes fastest.
Arguments:
- blocks: bfloat16 [24, 32, 12, 128, 128], P('row', 'col'), may hold values from -1 to 1, as said below
- block_row: int32 [24, 32, 12], P('row', 'col'), may hold values from -1 to 383, as said below
- block_col: int32 [24, 32, 12], P('row', 'col'), may hold values from -1 to 383, as said below
Outputs:
- factor: bfloat16 [24, 32, 12, 128, 128], P('row', 'col')
- trace: float32 [], replicated
Inputs may be any that keep to these rules, and one draw needn't show every extreme that they name: `block_row`: ids are -1 in exactly the empty slots. All filled blocks of one block row are held on one index of row, all filled blocks of one block column on one index of col. A slot is empty in block_col exactly where it is empty in block_row. `blocks`: X is symmetric: the block (j, i) is the transpose of the block (i, j). Empty slots hold arbitrary values.
All inputs are finite; a program needn't handle non-finite values.
Results may differ from a plain program's by a relative error of at most 0.001.
Values may be sent and summed in bfloat16 or wider, within the bound.
A program may use at most 128 MiB of HBM per device.

v0:
```python
import jax
import jax.numpy as jnp
from jax import lax
from jax.sharding import Mesh
from jax.sharding import PartitionSpec as P

HALF = 10
CPG = 12
COL = ("col_0", "col_1")
ROW = ("row_0", "row_1")
ROW_COL = ("row_0", "row_1", "col_0", "col_1")


def over_axes(x, axes):
    for axis in axes:
        x = lax.psum(x, axis)
    return x


def pair_product(own_rows, own_cols, left, right, bound):
    left_blocks, left_rows, left_cols = left
    right_blocks, right_rows, right_cols = right
    left_count = left_rows.shape[0]
    right_count = right_rows.shape[0]
    match = (
        (own_rows[:, None, None] >= 0)
        & (left_rows[None, :, None] == own_rows[:, None, None])
        & (left_rows[None, :, None] >= 0)
    )
    match = (
        match
        & (left_cols[None, :, None] == right_rows[None, None, :])
        & (right_rows[None, None, :] >= 0)
    )
    match = match & (right_cols[None, None, :] == own_cols[:, None, None])
    chosen = jnp.sum(jnp.where(match, jnp.arange(right_count, dtype=jnp.int32), 0), axis=2)
    hit = jnp.any(match, axis=2)
    ranked = jnp.cumsum(hit.astype(jnp.int32), axis=1) - 1
    width = min(bound, left_count)
    places = jnp.arange(width, dtype=jnp.int32)
    select = hit[:, None, :] & (ranked[:, None, :] == places[None, :, None])
    left_index = jnp.sum(
        jnp.where(select, jnp.arange(left_count, dtype=jnp.int32)[None, None, :], 0), axis=2
    )
    right_index = jnp.sum(jnp.where(select, chosen[:, None, :], 0), axis=2)
    used = jnp.any(select, axis=2)
    left_pick = jnp.where(used[:, :, None, None], left_blocks[left_index], 0)
    right_pick = jnp.where(used[:, :, None, None], right_blocks[right_index], 0)
    return jnp.einsum("spxy,spyz->sxz", left_pick, right_pick, preferred_element_type=jnp.float32)


def shards(blocks, block_row, block_col):
    order = blocks.shape[3]
    pairs = 2 * HALF + 1
    matrix_blocks = CPG * lax.axis_size(COL)
    own_blocks = blocks[0, 0]
    own_rows = block_row[0, 0]
    own_cols = block_col[0, 0]
    right = (
        lax.all_gather(own_blocks, ROW, axis=0, tiled=True),
        lax.all_gather(own_rows, ROW, axis=0, tiled=True),
        lax.all_gather(own_cols, ROW, axis=0, tiled=True),
    )
    left = (
        lax.all_gather(own_blocks, COL, axis=0, tiled=True),
        lax.all_gather(own_rows, COL, axis=0, tiled=True),
        lax.all_gather(own_cols, COL, axis=0, tiled=True),
    )
    square = pair_product(own_rows, own_cols, left, right, pairs)
    diagonal = ((own_rows == own_cols) & (own_rows >= 0)).astype(jnp.float32)
    identity = jnp.eye(order, dtype=jnp.float32)
    factor = (1.5 * diagonal[:, None, None] * identity - 0.5 * square).astype(jnp.bfloat16)
    part = jnp.sum(diagonal * jnp.trace(square, axis1=1, axis2=2))
    trace = over_axes(part, ROW_COL) / (matrix_blocks * order)
    return (factor[None, None], trace)


def solution(mesh):
    torus = Mesh(mesh.devices.reshape(12, 2, 4, 8), ("row_0", "row_1", "col_0", "col_1"))
    in_specs = (P(ROW, COL, None, None, None), P(ROW, COL, None), P(ROW, COL, None))
    out_specs = (P(ROW, COL, None, None, None), P())
    return jax.shard_map(
        shards, mesh=torus, in_specs=in_specs, out_specs=out_specs, check_vma=False
    )
```

profile of v0, /device:TPU:2, one launch (start us, length us, event | category | flops | bytes accessed | tf_op | source)
XLA Modules:
  0.0 304.3 jit_solution(2242097978642386079)
XLA Ops:
  7.2 0.7 all-gather.11.cloned.1.call-update
  7.9 0.7 all-gather.9.cloned.1.call-update
  8.7 1.3 dynamic-slice
  9.9 1.3 dynamic-slice.2
  12.5 0.8 bitcast_dynamic-update-slice_fusion.3
  13.3 0.8 bitcast_dynamic-update-slice_fusion.1
  14.0 20.6 %all-reduce.4 = (s32[384]{0:T(512)S(1)}, s32[384]{0:T(512)S(1)}) all-reduce(s32[384]{0:T(512)S(1)} %get-tuple-element.12, s32[384]{0:T(512)S(1)} %get-tuple-element.10), channel_id=3, replica_groups=mesh['row_0'=12,'row_1'=2,'col_0'=4,'col_1'=8] {'col_0','col_1'}, use_global_device_ids=true, to_apply=%add.1 | all-reduce | flops 768 | bytes 6144
  34.7 46.9 %all-reduce.5 = (s32[288]{0:T(512)S(1)}, s32[288]{0:T(512)S(1)}) all-reduce(s32[288]{0:T(512)S(1)} %get-tuple-element.11, s32[288]{0:T(512)S(1)} %get-tuple-element.13), channel_id=4, replica_groups=mesh['row_0'=12,'row_1'=2,'col_0'=4,'col_1'=8] {'row_0','row_1'}, use_global_device_ids=true, to_apply=%add.2 | all-reduce | flops 576 | bytes 4608 | tf_op jit(solution)/shard_map/all_gather | solution.py:61
  81.6 0.7 broadcast_compare_fusion.4
  82.2 0.7 broadcast_compare_fusion.1
  83.0 0.7 and_and_fusion.1
  83.8 1.3 fusion.4
  85.2 0.9 reduce-window.6
  86.4 1.8 select_reduce_fusion
  89.3 0.7 broadcast_select_fusion
  90.0 12.3 %gather_fusion.1 = bf16[252,128,128]{2,1,0:T(8,128)(2,1)} fusion(bf16[288,128,128]{2,1,0:T(8,128)(2,1)} %bitcast.46, s32[1024]{0:T(1024)S(1)} %pad_clamp_fusion), kind=kCustom, calls=%fused_computation.1 | custom fusion | bytes 16516080 | tf_op jit(solution)/shard_map/gather | solution.py:48
  102.3 115.3 %all-gather.9.cloned.1.call-done = bf16[1,1,384,128,128]{4,3,1,0,2:T(8,128)(2,1)} async-done(((bf16[1,1,12,128,128]{4,3,1,0,2:T(8,128)(2,1)}), bf16[1,1,384,128,128]{4,3,1,0,2:T(8,128)(2,1)}) %all-gather.9.cloned.1.call-update) | async-done | bytes 12582928 | tf_op jit(solution)/shard_map/all_gather | solution.py:65
  217.6 13.1 %gather_fusion = bf16[252,128,128]{2,1,0:T(8,128)(2,1)} fusion(bf16[384,128,128]{2,1,0:T(8,128)(2,1)} %bitcast.47, s32[1024]{0:T(1024)S(1)} %pad_clamp_fusion.1), kind=kCustom, calls=%fused_computation | custom fusion | bytes 16516080 | tf_op jit(solution)/shard_map/gather | solution.py:47
  230.7 9.1 %select_reduce_fusion.1 = (f32[12]{0:T(128)S(1)}, bf16[1,1,12,128,128]{4,3,2,1,0:T(8,128)(2,1)}) fusion(pred[128,128]{1,0:T(8,128)(4,1)S(1)} %get-tuple-element.16, f32[128,128]{1,0:T(8,128)S(1)} %get-tuple-element.17, f32[12]{0:T(128)S(1)} %broadcast_select_fusion, bf16[12,21,128,128]{3,2,1,0:T(8,128)(2,1)} %bitcast.44, pred[12,21]{1,0:T(8,128)(4,1)S(1)} %fusion.12, ...), kind=kOutput, calls=%fused_computation.11 | convolution fusion | flops 1066401792 | bytes 16990556 | tf_op jit(solution)/shard_map/spxy,spyz->sxz/dot_general | solution.py:49
  239.8 0.6 select_reduce_fusion.4
  240.4 25.9 %psum.28 = f32[]{:T(128)} all-reduce(f32[]{:T(128)} %select_reduce_fusion.4), channel_id=1, replica_groups=mesh['row_0'=12,'row_1'=2,'col_0'=4,'col_1'=8] {'row_0'}, use_global_device_ids=true, to_apply=%region_9.10 | all-reduce | flops 1 | bytes 8 | tf_op jit(solution)/shard_map/psum | solution.py:16
  266.3 3.1 %psum.29 = f32[]{:T(128)} all-reduce(f32[]{:T(128)} %psum.28), channel_id=1, replica_groups=mesh['row_0'=12,'row_1'=2,'col_0'=4,'col_1'=8] {'row_1'}, use_global_device_ids=true, to_apply=%region_10.11 | all-reduce | flops 1 | bytes 8 | tf_op jit(solution)/shard_map/psum | solution.py:16
  269.4 10.2 %psum.30 = f32[]{:T(128)} all-reduce(f32[]{:T(128)} %psum.29), channel_id=1, replica_groups=mesh['row_0'=12,'row_1'=2,'col_0'=4,'col_1'=8] {'col_0'}, use_global_device_ids=true, to_apply=%region_11.12 | all-reduce | flops 1 | bytes 8 | tf_op jit(solution)/shard_map/psum | solution.py:16
  279.5 16.2 %psum.31 = f32[]{:T(128)} all-reduce(f32[]{:T(128)} %psum.30), channel_id=1, replica_groups=mesh['row_0'=12,'row_1'=2,'col_0'=4,'col_1'=8] {'col_1'}, use_global_device_ids=true, to_apply=%region_12.13 | all-reduce | flops 1 | bytes 8 | tf_op jit(solution)/shard_map/psum | solution.py:16
  (31 shorter events, 1.6 us)
Async XLA Ops:
  7.2 82.8 %all-gather.11.cloned.1.call-start = ((), (), s32[]{:S(2)}) async-start(), calls=%async_computation.1 | async-start | bytes 9830400 | tf_op jit(solution)/shard_map/all_gather | solution.py:60
  7.9 209.7 %all-gather.9.cloned.1.call-start = ((), (), s32[]{:S(2)}) async-start(), calls=%async_computation | async-start | bytes 12976128 | tf_op jit(solution)/shard_map/all_gather | solution.py:65
  230.7 9.1 %copy-start = (s32[1,1,12]{2,1,0:T(1,128)S(1)}, s32[1,1,12]{2,1,0:T(1,128)}, u32[]{:S(2)}) copy-start(s32[1,1,12]{2,1,0:T(1,128)} %param.5) | copy-start | bytes 148
  230.7 9.1 %copy-start.1 = (s32[1,1,12]{2,1,0:T(1,128)S(1)}, s32[1,1,12]{2,1,0:T(1,128)}, u32[]{:S(2)}) copy-start(s32[1,1,12]{2,1,0:T(1,128)} %param.4) | copy-start | bytes 148
Sparse Core Ops, SparseCore 0:
  10.4 77.5 all-gather.10
  91.8 125.8 all-gather.8
where the time goes:
time: 305 us; the launch traced here: 304 us
  blocking collectives  123 us (40%)
  waiting for transfers between devices  117 us (38%)
  local copies, waits for them, and re-layouts  29.9 us (10%)
  between operations  17.3 us (6%)
  matrix products  9.12 us (3%)
  other arithmetic  8.45 us (3%)
    all_gather x1, waiting for transfers between devices, shards(): lax.all_gather(own_blocks, COL, axis=0, tiled=True)  115 us
    psum x4, blocking collectives, over_axes(): x = lax.psum(x, axis)  55.3 us
    all_gather x1, blocking collectives, shards(): lax.all_gather(own_rows, ROW, axis=0, tiled=True)  46.9 us
    unnamed x1, blocking collectives  20.6 us
    gather x1, local copies, waits for them, and re-layouts, pair_product(): left_pick = jnp.where(used[:, :, None, None], left_blocks[left_index], 0)  13.1 us
    gather x1, local copies, waits for them, and re-layouts, pair_product(): right_pick = jnp.where(used[:, :, None, None], right_blocks[right_index], 0)  12.3 us
    dot_general x1, matrix products, pair_product(): jnp.einsum('spxy,spyz->sxz', left_pick, right_pick, preferred_element_typ...  9.12 us
  transfers between devices with their start and end apart: 2, of which 1 were waited for; matrix products, arithmetic and copies ran while one was open for 8% of the time, Pallas kernels for 0%

commit v1 on v0

v1 whole, which is shorter than its diff:
```python
import functools
import heapq

import jax
import jax.numpy as jnp
from jax import lax
from jax.experimental import pallas as pl
from jax.experimental.pallas import tpu as pltpu
from jax.sharding import Mesh
from jax.sharding import PartitionSpec as P

HALF = 10
PAIRS = 2 * HALF + 1
QUERIES = 24
SLOTS = 12
BS = 128
NB = 384
AXES = ("z", "core", "x", "y")
NZ, NCORE, NX, NY = 12, 2, 4, 8
COL = ("x", "y")
ROW = ("z", "core")
MESH = pl.DeviceIdType.MESH

PART_A = 5
BODY = SLOTS * BS
LEFT_ROWS = BODY
SUMS = BODY
RIGHT_ROWS = BODY + 16
NOTHING = NB * NB
N_LEFT, N_RIGHT = NX * NY, NZ * NCORE
LEFT_ZERO = N_LEFT * LEFT_ROWS
RIGHT_ZERO = N_RIGHT * RIGHT_ROWS


def plan():
    size, need, rows = {}, {}, {}

    def add(name, link, first, last, after):
        size[name] = (link, (last - first) / BS)
        need[name] = after
        rows[name] = (first, last - first)

    cut = PART_A * BS
    add(("AX", "R", 1), "xR", 0, cut, [])
    add(("AX", "L", 1), "xL", 0, cut, [])
    add(("AX", "R", 2), "xR", 0, 2 * BS, [("AX", "R", 1)])
    add(("AX", "L", 2), "xL", 2 * BS, cut, [("AX", "L", 1)])
    came = {0: [], -1: [("AX", "R", 1)], 1: [("AX", "L", 1)], 2: [("AX", "R", 2), ("AX", "L", 2)]}
    for d in "UD":
        add(("BY", d, 1), "y" + d, cut, LEFT_ROWS, [])
        for h in (2, 3):
            add(("BY", d, h), "y" + d, cut, LEFT_ROWS, [("BY", d, h - 1)])
    add(("BY", "U", 4), "yU", cut, 8 * BS, [("BY", "U", 3)])
    add(("BY", "D", 4), "yD", 8 * BS, LEFT_ROWS, [("BY", "D", 3)])
    for dx in (0, -1, 1, 2):
        for d in "UD":
            add(("AY", d, 1, dx), "y" + d, 0, cut, came[dx])
            for h in (2, 3):
                add(("AY", d, h, dx), "y" + d, 0, cut, [("AY", d, h - 1, dx)])
        d = "U" if dx in (0, -1) else "D"
        add(("AY", d, 4, dx), "y" + d, 0, cut, [("AY", d, 3, dx)])
    came = {0: [], 4: [("BY", "U", 4), ("BY", "D", 4)]}
    for h in (1, 2, 3):
        came[-h], came[h] = [("BY", "U", h)], [("BY", "D", h)]
    for dy in (0, -1, 1, -2, 2, -3, 3, 4):
        for d in "RL":
            add(("BX", d, 1, dy), "x" + d, cut, LEFT_ROWS, came[dy])
        d = "R" if dy in (0, -1, 2, -3) else "L"
        add(("BX", d, 2, dy), "x" + d, cut, LEFT_ROWS, [("BX", d, 1, dy)])
    add(("CX", "R", 1), "xR", 0, 1, [])
    add(("CX", "L", 1), "xL", 0, 1, [])
    add(("CX", "R", 2), "xR", 0, 1, [("CX", "R", 1)])
    for d in "UD":
        for h in range(1, 5 if d == "U" else 4):
            after = [("CY", d, h - 1)] if h > 1 else [("CX", "R", 1), ("CX", "L", 1), ("CX", "R", 2)]
            add(("CY", d, h), "y" + d, 0, NX, after)
    add(("CS", "O", 0), "s", 0, 1, [])
    for d in "UD":
        for h in range(1, 7 if d == "U" else 6):
            add(("CZ", d, h), "z" + d, 0, NCORE, [("CZ", d, h - 1)] if h > 1 else [("CS", "O", 0)])
    half = BODY // 2
    for d in "UD":
        for h in range(1, 6):
            add(("ZZ", d, h), "z" + d, 0, RIGHT_ROWS, [("ZZ", d, h - 1)] if h > 1 else [])
    add(("ZZ", "U", 6), "zU", 0, half, [("ZZ", "U", 5)])
    add(("ZZ", "D", 6), "zD", half, RIGHT_ROWS, [("ZZ", "D", 5)])
    add(("SS", "O", 0), "s", 0, RIGHT_ROWS, [])
    for d in "UD":
        for h in range(1, 7):
            first, count = rows[("ZZ", d, h)]
            add(("SS", d, h), "s", first, first + count, [("ZZ", d, h)])
    return size, need, rows


def expected(size, need):
    rank = {"CX": -4, "CS": -3, "CY": -2, "CZ": -1, "AX": 0, "BY": 1, "AY": 2, "BX": 3, "ZZ": 4, "SS": 5}
    free, queue, order = {}, [], []
    pending = {m: set(after) for m, after in need.items()}

    def issue(m, now):
        link, blocks = size[m]
        free[link] = max(now, free.get(link, 0.0)) + blocks * (0.18 if link == "s" else 0.7)
        heapq.heappush(queue, (round(free[link] + 1.6, 6), len(order), list(size).index(m), m))

    first = sorted((m for m in size if not need[m]), key=lambda m: rank[m[0]])
    for m in first:
        issue(m, 0.0)
    while queue:
        now, _, _, m = heapq.heappop(queue)
        released = []
        for other, waits in pending.items():
            if m in waits:
                waits.discard(m)
                if not waits:
                    released.append(other)
        released.sort(key=lambda n: rank[n[0]])
        for other in released:
            issue(other, now)
        order.append((m, released))
    return first, order


SIZE, NEED, ROWS = plan()
FIRST, ORDER = expected(SIZE, NEED)
INDEX = {m: i for i, m in enumerate(SIZE)}
N_BULK = len(SIZE)
N_SEM = N_BULK + NX - 1 + NY - 1


def kernel(
    blocks, row_ids, col_ids, factor, trace, left, right, left_ids, right_ids, x_sums, y_sums, left_at, right_at,
    left_look, right_look, send, recv, local,
):
    z, core, x, y = (lax.axis_index(a) for a in AXES)

    def at(base, shift, extent):
        return lax.rem(base + (shift + extent), extent)

    def left_chunk(dx, dy):
        return (at(x, dx, NX) * NY + at(y, dy, NY)) * LEFT_ROWS

    def right_chunk(dz, which):
        return (at(z, dz, NZ) * NCORE + which) * RIGHT_ROWS

    def near(axis, shift):
        base, extent = {"x": (x, NX), "y": (y, NY), "z": (z, NZ)}[axis]
        return {axis: at(base, shift, extent)}

    own_left = left_chunk(0, 0)
    own_right = right_chunk(0, core)
    mine = [
        pltpu.make_async_copy(
            blocks, left.at[pl.ds(pl.multiple_of(own_left, 16), BODY), :], local.at[0]
        ),
        pltpu.make_async_copy(
            blocks, right.at[pl.ds(pl.multiple_of(own_right, 16), BODY), :], local.at[1]
        ),
    ]
    for copy in mine:
        copy.start()

    barrier = pltpu.get_barrier_semaphore()
    partners = [near(a, s) for a in ("x", "y", "z") for s in (1, -1)] + [{"core": 1 - core}]
    for partner in partners:
        pl.semaphore_signal(barrier, inc=1, device_id=partner, device_id_type=MESH)

    lane = lax.broadcasted_iota(jnp.int32, (1, BS), 1)
    code = jnp.full((1, BS), NOTHING, jnp.int32)
    for t in range(SLOTS):
        value = jnp.where(row_ids[t] >= 0, row_ids[t] * NB + col_ids[t], NOTHING)
        code = jnp.where(lane == t, value, code)
    left_ids[y * NX + x] = code
    right_ids[z * NCORE + core] = code
    left[pl.ds(LEFT_ZERO, BS), :] = jnp.zeros((BS, BS), jnp.bfloat16)
    right[pl.ds(RIGHT_ZERO, BS), :] = jnp.zeros((BS, BS), jnp.bfloat16)

    for copy in mine:
        copy.wait()

    total = jnp.zeros((8, BS), jnp.float32)
    for t in range(SLOTS):
        block = left[pl.ds(pl.multiple_of(own_left + t * BS, 16), BS), :].astype(jnp.float32)
        folded = jnp.sum((block * block).reshape(BS // 8, 8, BS), axis=0)
        total = total + jnp.where(row_ids[t] >= 0, folded, 0.0)
    part = jnp.sum(jnp.sum(total, axis=1, keepdims=True), axis=0, keepdims=True)
    high = part.astype(jnp.bfloat16).astype(jnp.float32)
    middle = (part - high).astype(jnp.bfloat16).astype(jnp.float32)
    low = part - high - middle
    row_iota = lax.broadcasted_iota(jnp.int32, (16, BS), 0)
    piece = jnp.where(row_iota == 0, high, jnp.where(row_iota == 1, middle, low))
    right[pl.ds(pl.multiple_of(own_right + SUMS, 16), 16), :] = jnp.where(
        row_iota < 3, piece, 0.0
    ).astype(jnp.bfloat16)

    pl.semaphore_wait(barrier, len(partners))

    def transfer(m):
        kind, d, h = m[:3]
        first, count = ROWS[m]
        sign = -1 if d in "RU" else 1
        step = sign * (h - 1)
        if kind in ("CX", "CY"):
            ref = left_ids
            where = y * NX + at(x, step, NX) if kind == "CX" else at(y, step, NY) * NX
            target = near(kind[1].lower(), -sign)
        elif kind in ("CS", "CZ"):
            ref = right_ids
            where = z * NCORE + core if kind == "CS" else at(z, step, NZ) * NCORE
            target = {"core": 1 - core} if kind == "CS" else near("z", -sign)
        elif kind in ("ZZ", "SS"):
            if kind == "SS":
                where = right_chunk(sign * h if h else 0, core)
                target = {"core": 1 - core}
            else:
                where = right_chunk(step, core)
                target = near("z", -sign)
            ref = right
        else:
            if kind == "AX":
                where = left_chunk(step, 0)
            elif kind == "BX":
                where = left_chunk(step, m[3])
            elif kind == "BY":
                where = left_chunk(0, step)
            else:
                where = left_chunk(m[3], step)
            target = near("x" if kind in ("AX", "BX") else "y", -sign)
            ref = left
        if kind[0] == "C":
            view = ref.at[pl.ds(where, count)]
        else:
            view = ref.at[pl.ds(pl.multiple_of(where + first, 16), count), :]
        i = INDEX[m]
        return pltpu.make_async_remote_copy(
            src_ref=view, dst_ref=view, send_sem=send.at[i], recv_sem=recv.at[i],
            device_id=target, device_id_type=MESH,
        )

    def sum_transfer(axis, k):
        ref, here = (x_sums, x) if axis == "x" else (y_sums, y)
        i = N_BULK + (k - 1 if axis == "x" else NX - 1 + k - 1)
        return pltpu.make_async_remote_copy(
            src_ref=ref.at[here], dst_ref=ref.at[here], send_sem=send.at[i], recv_sem=recv.at[i],
            device_id=near(axis, k), device_id_type=MESH,
        )

    query = lax.broadcasted_iota(jnp.int32, (QUERIES, BS), 0)
    spread = query == lax.broadcasted_iota(jnp.int32, (QUERIES, BS), 1)
    slot_of_lane = lax.broadcasted_iota(jnp.int32, (1, BS), 1) * (BS // 16)

    def look_up(ids, n, chunk_of, nothing, table, by_row):
        def one(s, carry):
            i, j = row_ids[s], col_ids[s]
            k = i - HALF + query
            k = jnp.where(k < 0, k + NB, jnp.where(k >= NB, k - NB, k))
            gap = jnp.abs(k - j)
            gap = jnp.minimum(gap, NB - gap)
            wanted = i * NB + k if by_row else k * NB + j
            wanted = jnp.where((query < PAIRS) & (gap <= HALF) & (i >= 0), wanted, -1)
            found = jnp.full((QUERIES, BS), -1, jnp.int32)
            for c in range(n):
                found = jnp.where(wanted == ids[c], slot_of_lane + chunk_of(c), found)
            found = jnp.max(found, axis=1, keepdims=True)
            found = jnp.where(found < 0, nothing, found)
            table[pl.ds(s, 1), :] = jnp.max(jnp.where(spread, found, 0), axis=0, keepdims=True)
            return carry

        lax.fori_loop(0, SLOTS, one, 0)

    for m in FIRST:
        transfer(m).start()
    last_right = max(i for i, (m, _) in enumerate(ORDER) if m[0] in ("ZZ", "SS"))
    for i, (m, released) in enumerate(ORDER):
        transfer(m).wait_recv()
        for other in released:
            transfer(other).start()
        if i == last_right:
            total = jnp.zeros((16, BS), jnp.float32)
            for c in range(N_RIGHT):
                total = total + right[pl.ds(c * RIGHT_ROWS + SUMS, 16), :].astype(jnp.float32)
            x_sums[x] = jnp.broadcast_to(jnp.sum(total, axis=0, keepdims=True), (8, BS))
            look_up(right_ids, N_RIGHT, lambda c: c * (RIGHT_ROWS // 16), RIGHT_ZERO // 16, right_at, False)
            for k in range(1, NX):
                sum_transfer("x", k).start()
        if i == min(last_right + 6, len(ORDER) - 1):
            for k in range(1, NX):
                sum_transfer("x", k).wait_recv()
            total = x_sums[0]
            for k in range(1, NX):
                total = total + x_sums[k]
            y_sums[y] = total
        if i == min(last_right + 8, len(ORDER) - 1):
            for k in range(1, NY):
                sum_transfer("y", k).start()
    look_up(
        left_ids, N_LEFT, lambda c: (c % NX * NY + c // NX) * (LEFT_ROWS // 16), LEFT_ZERO // 16, left_at, True
    )
    for k in range(1, NY):
        sum_transfer("y", k).wait_recv()
    total = y_sums[0]
    for k in range(1, NY):
        total = total + y_sums[k]
    trace[...] = total * (1.0 / (NB * BS))

    looks = [
        pltpu.make_async_copy(left_at, left_look, local.at[0]),
        pltpu.make_async_copy(right_at, right_look, local.at[1]),
    ]
    for copy in looks:
        copy.start()
    for copy in looks:
        copy.wait()

    eye = lax.broadcasted_iota(jnp.int32, (BS, BS), 0) == lax.broadcasted_iota(jnp.int32, (BS, BS), 1)

    def one_slot(s, carry):
        def fetch(ref, table, q):
            return ref[pl.ds(table[s, q] * 16, BS), :]

        square = jnp.zeros((BS, BS), jnp.float32)
        for q in range(0, PAIRS + 1, 2):
            a = jnp.concatenate([fetch(left, left_look, q), fetch(left, left_look, q + 1)], axis=1)
            b = jnp.concatenate([fetch(right, right_look, q), fetch(right, right_look, q + 1)], axis=0)
            square = square + jnp.dot(a, b, preferred_element_type=jnp.float32)
        scale = jnp.where((row_ids[s] == col_ids[s]) & (row_ids[s] >= 0), 1.5, 0.0)
        factor[s] = (jnp.where(eye, scale, 0.0) - 0.5 * square).astype(jnp.bfloat16)
        return carry

    lax.fori_loop(0, SLOTS, one_slot, 0)

    for m in SIZE:
        transfer(m).wait_send()
    for axis, extent in (("x", NX), ("y", NY)):
        for k in range(1, extent):
            sum_transfer(axis, k).wait_send()


def shards(blocks, block_row, block_col):
    smem = pl.BlockSpec(memory_space=pltpu.SMEM)
    vmem = pl.BlockSpec(memory_space=pltpu.VMEM)
    factor, trace = pl.pallas_call(
        kernel,
        out_shape=(
            jax.ShapeDtypeStruct((SLOTS, BS, BS), jnp.bfloat16),
            jax.ShapeDtypeStruct((8, BS), jnp.float32),
        ),
        in_specs=[pl.BlockSpec(memory_space=pl.ANY), smem, smem],
        out_specs=(vmem, vmem),
        scratch_shapes=[
            pltpu.VMEM((LEFT_ZERO + BS, BS), jnp.bfloat16),
            pltpu.VMEM((RIGHT_ZERO + BS, BS), jnp.bfloat16),
            pltpu.VMEM((N_LEFT, 1, BS), jnp.int32),
            pltpu.VMEM((N_RIGHT, 1, BS), jnp.int32),
            pltpu.VMEM((NX, 8, BS), jnp.float32),
            pltpu.VMEM((NY, 8, BS), jnp.float32),
            pltpu.VMEM((16, BS), jnp.int32),
            pltpu.VMEM((16, BS), jnp.int32),
            pltpu.SMEM((16, BS), jnp.int32),
            pltpu.SMEM((16, BS), jnp.int32),
            pltpu.SemaphoreType.DMA((N_SEM,)),
            pltpu.SemaphoreType.DMA((N_SEM,)),
            pltpu.SemaphoreType.DMA((2,)),
        ],
        compiler_params=pltpu.CompilerParams(collective_id=0, has_side_effects=True),
    )(blocks.reshape(BODY, BS), block_row.reshape(SLOTS), block_col.reshape(SLOTS))
    return factor[None, None], trace[0, 0]


def solution(mesh):
    torus = Mesh(mesh.devices.reshape(NZ, NCORE, NX, NY), AXES)
    return jax.shard_map(
        shards,
        mesh=torus,
        in_specs=(P(ROW, COL, None, None, None), P(ROW, COL, None), P(ROW, COL, None)),
        out_specs=(P(ROW, COL, None, None, None), P()),
        check_vma=False,
    )
```

time: 305 us -> 102 us (0.33)
  blocking collectives: 123 us -> 0 us
  waiting for transfers between devices: 117 us -> 0 us
  Pallas kernels: 0 us -> 98 us
  local copies, waits for them, and re-layouts: 29.9 us -> 2.95 us
  between operations: 17.3 us -> 0.64 us
  matrix products: 9.12 us -> 0 us
  other arithmetic: 8.45 us -> 0 us
    all_gather x2 -> x0, waiting for transfers between devices: 115 us -> none  [the longest x1 115 us: shards(): lax.all_gather(own_blocks, COL, axis=0, tiled=True)]
    pallas_call x0 -> x1, Pallas kernels: none -> 98 us  [shards(): pl.pallas_call(kernel, out_shape=(jax.ShapeDtypeStruct((SLOTS, BS, BS), j...]
    psum x4 -> x0, blocking collectives: 55.3 us -> none  [over_axes(): x = lax.psum(x, axis)]
    all_gather x1 -> x0, blocking collectives: 46.9 us -> none  [shards(): lax.all_gather(own_rows, ROW, axis=0, tiled=True)]
    gather x2 -> x0, local copies, waits for them, and re-layouts: 25.4 us -> none  [the longest x1 13.1 us: pair_product(): left_pick = jnp.where(used[:, :, None, None], left_blocks[left_index], 0)]
    unnamed x1 -> x0, blocking collectives: 20.6 us -> none
    dot_general x1 -> x0, matrix products: 9.12 us -> none  [pair_product(): jnp.einsum('spxy,spyz->sxz', left_pick, right_pick, preferred_element_typ...]
  transfers between devices with their start and end apart: 2 -> 0, of which waited for: 1 -> 0; matrix products, arithmetic and copies ran while one was open for 8% -> 0% of each run, Pallas kernels for 0% -> 0%
where the time goes in v1:
time: 102 us
  Pallas kernels  98 us (96%)
  local copies, waits for them, and re-layouts  2.95 us (3%)
    pallas_call x1, Pallas kernels, shards(): pl.pallas_call(kernel, out_shape=(jax.ShapeDtypeStruct((SLOTS, BS, BS), j...  98 us

profile of v1, /device:TPU:2, one launch (start us, length us, event | category | flops | bytes accessed | tf_op | source)
XLA Modules:
  0.0 101.6 jit_solution(16958011606271160100)
XLA Ops:
  0.6 98.0 %shard_map.50 = (bf16[12,128,128]{2,1,0:T(8,128)(2,1)}, f32[8,128]{1,0:T(8,128)}) custom-call(bf16[1536,128]{1,0:T(8,128)(2,1)} %bitcast.5, s32[12]{0:T(128)} %bitcast.7, s32[12]{0:T(128)} %bitcast.8), custom_call_target="tpu_custom_call" | custom-call | tf_op jit(solution)/shard_map/pallas_call | solution.py:341
  98.7 1.2 %slice.3 = f32[1,1]{1,0:T(1,128)} slice(f32[8,128]{1,0:T(8,128)} %get-tuple-element.5), slice={[0:1], [0:1]} | slice | bytes 8 | tf_op jit(solution)/shard_map/slice | solution.py:366
  99.8 1.8 %copy.6 = bf16[1,1,12,128,128]{4,3,2,1,0:T(8,128)(2,1)} copy(bf16[1,1,12,128,128]{4,3,2,1,0:T(8,128)(2,1)} %bitcast.6) | data formatting | bytes 786432

commit v2 on v1

--- a/solution.py
+++ b/solution.py
@@ -21,7 +21,10 @@
 ROW = ("z", "core")
 MESH = pl.DeviceIdType.MESH
 
-PART_A = 5
+PART_A = (2, 3)
+PART_B = (3, 4)
+PART_Z = (6, 6)
+BACKLOG = 4.0
 BODY = SLOTS * BS
 LEFT_ROWS = BODY
 SUMS = BODY
@@ -35,88 +38,114 @@
 def plan():
     size, need, rows = {}, {}, {}
 
-    def add(name, link, first, last, after):
-        size[name] = (link, (last - first) / BS)
+    def add(name, link, span, after):
+        size[name] = (link, (span[1] - span[0]) / BS)
         need[name] = after
-        rows[name] = (first, last - first)
-
-    cut = PART_A * BS
-    add(("AX", "R", 1), "xR", 0, cut, [])
-    add(("AX", "L", 1), "xL", 0, cut, [])
-    add(("AX", "R", 2), "xR", 0, 2 * BS, [("AX", "R", 1)])
-    add(("AX", "L", 2), "xL", 2 * BS, cut, [("AX", "L", 1)])
-    came = {0: [], -1: [("AX", "R", 1)], 1: [("AX", "L", 1)], 2: [("AX", "R", 2), ("AX", "L", 2)]}
-    for d in "UD":
-        add(("BY", d, 1), "y" + d, cut, LEFT_ROWS, [])
-        for h in (2, 3):
-            add(("BY", d, h), "y" + d, cut, LEFT_ROWS, [("BY", d, h - 1)])
-    add(("BY", "U", 4), "yU", cut, 8 * BS, [("BY", "U", 3)])
-    add(("BY", "D", 4), "yD", 8 * BS, LEFT_ROWS, [("BY", "D", 3)])
-    for dx in (0, -1, 1, 2):
+        rows[name] = (span[0], span[1] - span[0])
+
+    def spans(parts, first):
+        for count in parts:
+            yield (first * BS, (first + count) * BS)
+            first += count
+
+    for p, span in enumerate(spans(PART_A, 0)):
+        for d in "RL":
+            add(("AX", d, 1, 0, p), "x" + d, span, [])
+        d = "RL"[p % 2]
+        add(("AX", d, 2, 0, p), "x" + d, span, [("AX", d, 1, 0, p)])
+        came = {0: [], -1: [("AX", "R", 1, 0, p)], 1: [("AX", "L", 1, 0, p)], 2: [("AX", d, 2, 0, p)]}
+        for dx in (0, -1, 1, 2):
+            for d in "UD":
+                add(("AY", d, 1, dx, p), "y" + d, span, came[dx])
+                for h in (2, 3):
+                    add(("AY", d, h, dx, p), "y" + d, span, [("AY", d, h - 1, dx, p)])
+            d = "U" if (dx in (0, -1)) == (p % 2 == 0) else "D"
+            add(("AY", d, 4, dx, p), "y" + d, span, [("AY", d, 3, dx, p)])
+    for p, span in enumerate(spans(PART_B, sum(PART_A))):
         for d in "UD":
-            add(("AY", d, 1, dx), "y" + d, 0, cut, came[dx])
+            add(("BY", d, 1, 0, p), "y" + d, span, [])
             for h in (2, 3):
-                add(("AY", d, h, dx), "y" + d, 0, cut, [("AY", d, h - 1, dx)])
-        d = "U" if dx in (0, -1) else "D"
-        add(("AY", d, 4, dx), "y" + d, 0, cut, [("AY", d, 3, dx)])
-    came = {0: [], 4: [("BY", "U", 4), ("BY", "D", 4)]}
-    for h in (1, 2, 3):
-        came[-h], came[h] = [("BY", "U", h)], [("BY", "D", h)]
-    for dy in (0, -1, 1, -2, 2, -3, 3, 4):
-        for d in "RL":
-            add(("BX", d, 1, dy), "x" + d, cut, LEFT_ROWS, came[dy])
-        d = "R" if dy in (0, -1, 2, -3) else "L"
-        add(("BX", d, 2, dy), "x" + d, cut, LEFT_ROWS, [("BX", d, 1, dy)])
-    add(("CX", "R", 1), "xR", 0, 1, [])
-    add(("CX", "L", 1), "xL", 0, 1, [])
-    add(("CX", "R", 2), "xR", 0, 1, [("CX", "R", 1)])
+                add(("BY", d, h, 0, p), "y" + d, span, [("BY", d, h - 1, 0, p)])
+        d = "UD"[p % 2]
+        add(("BY", d, 4, 0, p), "y" + d, span, [("BY", d, 3, 0, p)])
+        came = {0: [], 4: [("BY", d, 4, 0, p)]}
+        for h in (1, 2, 3):
+            came[-h], came[h] = [("BY", "U", h, 0, p)], [("BY", "D", h, 0, p)]
+        for dy in (0, -1, 1, -2, 2, -3, 3, 4):
+            for d in "RL":
+                add(("BX", d, 1, dy, p), "x" + d, span, came[dy])
+            d = "R" if (dy in (0, -1, 2, -3)) == (p % 2 == 0) else "L"
+            add(("BX", d, 2, dy, p), "x" + d, span, [("BX", d, 1, dy, p)])
+    for p, span in enumerate(spans(PART_Z, 0)):
+        if p == len(PART_Z) - 1:
+            span = (span[0], RIGHT_ROWS)
+        add(("SS", "O", 0, 0, p), "s", span, [])
+        for d in "UD":
+            for h in range(1, 7 if d == "UD"[p % 2] else 6):
+                add(("ZZ", d, h, 0, p), "z" + d, span, [("ZZ", d, h - 1, 0, p)] if h > 1 else [])
+                add(("SS", d, h, 0, p), "s", span, [("ZZ", d, h, 0, p)])
+    add(("CX", "R", 1), "xR", (0, 1), [])
+    add(("CX", "L", 1), "xL", (0, 1), [])
+    add(("CX", "R", 2), "xR", (0, 1), [("CX", "R", 1)])
     for d in "UD":
         for h in range(1, 5 if d == "U" else 4):
             after = [("CY", d, h - 1)] if h > 1 else [("CX", "R", 1), ("CX", "L", 1), ("CX", "R", 2)]
-            add(("CY", d, h), "y" + d, 0, NX, after)
-    add(("CS", "O", 0), "s", 0, 1, [])
+            add(("CY", d, h), "y" + d, (0, NX), after)
+    add(("CS", "O", 0), "s", (0, 1), [])
     for d in "UD":
         for h in range(1, 7 if d == "U" else 6):
-            add(("CZ", d, h), "z" + d, 0, NCORE, [("CZ", d, h - 1)] if h > 1 else [("CS", "O", 0)])
-    half = BODY // 2
-    for d in "UD":
-        for h in range(1, 6):
-            add(("ZZ", d, h), "z" + d, 0, RIGHT_ROWS, [("ZZ", d, h - 1)] if h > 1 else [])
-    add(("ZZ", "U", 6), "zU", 0, half, [("ZZ", "U", 5)])
-    add(("ZZ", "D", 6), "zD", half, RIGHT_ROWS, [("ZZ", "D", 5)])
-    add(("SS", "O", 0), "s", 0, RIGHT_ROWS, [])
-    for d in "UD":
-        for h in range(1, 7):
-            first, count = rows[("ZZ", d, h)]
-            add(("SS", d, h), "s", first, first + count, [("ZZ", d, h)])
+            add(("CZ", d, h), "z" + d, (0, NCORE), [("CZ", d, h - 1)] if h > 1 else [("CS", "O", 0)])
     return size, need, rows
 
 
 def expected(size, need):
-    rank = {"CX": -4, "CS": -3, "CY": -2, "CZ": -1, "AX": 0, "BY": 1, "AY": 2, "BX": 3, "ZZ": 4, "SS": 5}
-    free, queue, order = {}, [], []
-    pending = {m: set(after) for m, after in need.items()}
-
-    def issue(m, now):
+    after = {m: [] for m in size}
+    for m, waits in need.items():
+        for other in waits:
+            after[other].append(m)
+    length = {}
+
+    def duration(m):
         link, blocks = size[m]
-        free[link] = max(now, free.get(link, 0.0)) + blocks * (0.18 if link == "s" else 0.7)
-        heapq.heappush(queue, (round(free[link] + 1.6, 6), len(order), list(size).index(m), m))
-
-    first = sorted((m for m in size if not need[m]), key=lambda m: rank[m[0]])
-    for m in first:
-        issue(m, 0.0)
+        return blocks * (0.05 if link == "s" else 0.706)
+
+    def chain(m):
+        if m not in length:
+            length[m] = 1.6 + duration(m) + max([chain(n) for n in after[m]], default=0.0)
+        return length[m]
+
+    number = {m: i for i, m in enumerate(size)}
+    rank = {m: (m[0][0] != "C", -chain(m), number[m]) for m in size}
+    pending = {m: set(waits) for m, waits in need.items()}
+    free, queue, waiting = {}, [], {}
+
+    def start(now):
+        started = []
+        for link in sorted(waiting):
+            ready = sorted(waiting[link], key=lambda m: rank[m])
+            while ready and (link == "s" or free.get(link, 0.0) - now < BACKLOG):
+                m = ready.pop(0)
+                free[link] = max(now, free.get(link, 0.0)) + duration(m)
+                heapq.heappush(queue, (round(free[link] + 1.6, 6), len(started), number[m], m))
+                started.append(m)
+            waiting[link] = ready
+        return started
+
+    def release(m):
+        waiting.setdefault(size[m][0], []).append(m)
+
+    for m in size:
+        if not need[m]:
+            release(m)
+    first, order, now = start(0.0), [], 0.0
     while queue:
-        now, _, _, m = heapq.heappop(queue)
-        released = []
-        for other, waits in pending.items():
-            if m in waits:
-                waits.discard(m)
-                if not waits:
-                    released.append(other)
-        released.sort(key=lambda n: rank[n[0]])
-        for other in released:
-            issue(other, now)
-        order.append((m, released))
+        when, _, _, m = heapq.heappop(queue)
+        now = max(now, when) + 0.05
+        for other in after[m]:
+            pending[other].discard(m)
+            if not pending[other]:
+                release(other)
+        order.append((m, start(now), now))
     return first, order
 
 
@@ -267,66 +296,76 @@
 
         lax.fori_loop(0, SLOTS, one, 0)
 
+    def last(kinds):
+        return max(i for i, (m, _, _) in enumerate(ORDER) if m[0] in kinds)
+
+    def later(i, by):
+        return next((n for n in range(i, len(ORDER)) if ORDER[n][2] >= ORDER[i][2] + by), len(ORDER) - 1)
+
+    ids_left, ids_right, all_right = last(("CX", "CY")), last(("CS", "CZ")), last(("ZZ", "SS"))
+    ids_known = max(ids_left, ids_right)
+    looks = [
+        pltpu.make_async_copy(left_at, left_look, local.at[0]),
+        pltpu.make_async_copy(right_at, right_look, local.at[1]),
+    ]
+    x_known = later(all_right, 9.0)
     for m in FIRST:
         transfer(m).start()
-    last_right = max(i for i, (m, _) in enumerate(ORDER) if m[0] in ("ZZ", "SS"))
-    for i, (m, released) in enumerate(ORDER):
+    for i, (m, started, _) in enumerate(ORDER):
         transfer(m).wait_recv()
-        for other in released:
+        for other in started:
             transfer(other).start()
-        if i == last_right:
+        if i == ids_left:
+            look_up(
+                left_ids, N_LEFT, lambda c: (c % NX * NY + c // NX) * (LEFT_ROWS // 16), LEFT_ZERO // 16, left_at, True
+            )
+        if i == ids_right:
+            look_up(right_ids, N_RIGHT, lambda c: c * (RIGHT_ROWS // 16), RIGHT_ZERO // 16, right_at, False)
+        if i == later(ids_known, 2.0):
+            for copy in looks:
+                copy.start()
+        if i == all_right:
             total = jnp.zeros((16, BS), jnp.float32)
             for c in range(N_RIGHT):
                 total = total + right[pl.ds(c * RIGHT_ROWS + SUMS, 16), :].astype(jnp.float32)
             x_sums[x] = jnp.broadcast_to(jnp.sum(total, axis=0, keepdims=True), (8, BS))
-            look_up(right_ids, N_RIGHT, lambda c: c * (RIGHT_ROWS // 16), RIGHT_ZERO // 16, right_at, False)
+        if i == later(all_right, 0.5):
             for k in range(1, NX):
                 sum_transfer("x", k).start()
-        if i == min(last_right + 6, len(ORDER) - 1):
+        if i == x_known:
             for k in range(1, NX):
                 sum_transfer("x", k).wait_recv()
             total = x_sums[0]
             for k in range(1, NX):
                 total = total + x_sums[k]
             y_sums[y] = total
-        if i == min(last_right + 8, len(ORDER) - 1):
+        if i == later(x_known, 0.5):
             for k in range(1, NY):
                 sum_transfer("y", k).start()
-    look_up(
-        left_ids, N_LEFT, lambda c: (c % NX * NY + c // NX) * (LEFT_ROWS // 16), LEFT_ZERO // 16, left_at, True
-    )
+    for copy in looks:
+        copy.wait()
+
+    eye = lax.broadcasted_iota(jnp.int32, (BS, BS), 0) == lax.broadcasted_iota(jnp.int32, (BS, BS), 1)
+
+    def one_slot(s, carry):
+        def fetch(ref, table, q):
+            return ref[pl.ds(table[s, q] * 16, BS), :]
+
+        a = jnp.concatenate([fetch(left, left_look, q) for q in range(PAIRS + 1)], axis=1)
+        b = jnp.concatenate([fetch(right, right_look, q) for q in range(PAIRS + 1)], axis=0)
+        square = jnp.dot(a, b, preferred_element_type=jnp.float32)
+        scale = jnp.where((row_ids[s] == col_ids[s]) & (row_ids[s] >= 0), 1.5, 0.0)
+        factor[s] = (jnp.where(eye, scale, 0.0) - 0.5 * square).astype(jnp.bfloat16)
+        return carry
+
+    lax.fori_loop(0, SLOTS, one_slot, 0, unroll=4)
+
     for k in range(1, NY):
         sum_transfer("y", k).wait_recv()
     total = y_sums[0]
     for k in range(1, NY):
         total = total + y_sums[k]
-    trace[...] = total * (1.0 / (NB * BS))
-
-    looks = [
-        pltpu.make_async_copy(left_at, left_look, local.at[0]),
-        pltpu.make_async_copy(right_at, right_look, local.at[1]),
-    ]
-    for copy in looks:
-        copy.start()
-    for copy in looks:
-        copy.wait()
-
-    eye = lax.broadcasted_iota(jnp.int32, (BS, BS), 0) == lax.broadcasted_iota(jnp.int32, (BS, BS), 1)
-
-    def one_slot(s, carry):
-        def fetch(ref, table, q):
-            return ref[pl.ds(table[s, q] * 16, BS), :]
-
-        square = jnp.zeros((BS, BS), jnp.float32)
-        for q in range(0, PAIRS + 1, 2):
-            a = jnp.concatenate([fetch(left, left_look, q), fetch(left, left_look, q + 1)], axis=1)
-            b = jnp.concatenate([fetch(right, right_look, q), fetch(right, right_look, q + 1)], axis=0)
-            square = square + jnp.dot(a, b, preferred_element_type=jnp.float32)
-        scale = jnp.where((row_ids[s] == col_ids[s]) & (row_ids[s] >= 0), 1.5, 0.0)
-        factor[s] = (jnp.where(eye, scale, 0.0) - 0.5 * square).astype(jnp.bfloat16)
-        return carry
-
-    lax.fori_loop(0, SLOTS, one_slot, 0)
+    trace[0, 0] = jnp.max(total) * (1.0 / (NB * BS))
 
     for m in SIZE:
         transfer(m).wait_send()
@@ -342,10 +381,10 @@
         kernel,
         out_shape=(
             jax.ShapeDtypeStruct((SLOTS, BS, BS), jnp.bfloat16),
-            jax.ShapeDtypeStruct((8, BS), jnp.float32),
+            jax.ShapeDtypeStruct((1, 1), jnp.float32),
         ),
         in_specs=[pl.BlockSpec(memory_space=pl.ANY), smem, smem],
-        out_specs=(vmem, vmem),
+        out_specs=(vmem, smem),
         scratch_shapes=[
             pltpu.VMEM((LEFT_ZERO + BS, BS), jnp.bfloat16),
             pltpu.VMEM((RIGHT_ZERO + BS, BS), jnp.bfloat16),

time: 102 us -> 96.9 us (0.950)
  the two profiles are of different devices: /device:TPU:2 before, /device:TPU:28 now
where the time goes in v2:
time: 96.9 us; the launch traced here: 96.7 us
  Pallas kernels  92.6 us (96%)
  between operations  2.39 us (2%)
  local copies, waits for them, and re-layouts  1.77 us (2%)
    pallas_call x1, Pallas kernels, shards(): pl.pallas_call(kernel, out_shape=(jax.ShapeDtypeStruct((SLOTS, BS, BS), j...  92.6 us

profile of v2, /device:TPU:28, one launch (start us, length us, event | category | flops | bytes accessed | tf_op | source)
XLA Modules:
  0.0 96.7 jit_solution(1536791697181657364)
XLA Ops:
  0.6 92.6 %shard_map.50 = (bf16[12,128,128]{2,1,0:T(8,128)(2,1)}, f32[1,1]{1,0:T(1,128)}) custom-call(bf16[1536,128]{1,0:T(8,128)(2,1)} %bitcast.5, s32[12]{0:T(128)} %bitcast.7, s32[12]{0:T(128)} %bitcast.8), custom_call_target="tpu_custom_call" | custom-call | tf_op jit(solution)/shard_map/pallas_call | solution.py:380
  93.2 1.8 %copy.7 = bf16[1,1,12,128,128]{4,3,2,1,0:T(8,128)(2,1)} copy(bf16[1,1,12,128,128]{4,3,2,1,0:T(8,128)(2,1)} %bitcast.6) | data formatting | bytes 786432

commit v3 on v2

--- a/solution.py
+++ b/solution.py
@@ -25,6 +25,7 @@
 PART_B = (3, 4)
 PART_Z = (6, 6)
 BACKLOG = 4.0
+Z_PATIENCE = 1.0
 BODY = SLOTS * BS
 LEFT_ROWS = BODY
 SUMS = BODY
@@ -126,7 +127,8 @@
             while ready and (link == "s" or free.get(link, 0.0) - now < BACKLOG):
                 m = ready.pop(0)
                 free[link] = max(now, free.get(link, 0.0)) + duration(m)
-                heapq.heappush(queue, (round(free[link] + 1.6, 6), len(started), number[m], m))
+                wait = 1.6 + Z_PATIENCE * (link[0] == "z")
+                heapq.heappush(queue, (round(free[link] + wait, 6), len(started), number[m], m))
                 started.append(m)
             waiting[link] = ready
         return started
@@ -309,10 +311,14 @@
         pltpu.make_async_copy(right_at, right_look, local.at[1]),
     ]
     x_known = later(all_right, 9.0)
+    leaving = [(m, 0.0) for m in FIRST]
     for m in FIRST:
         transfer(m).start()
-    for i, (m, started, _) in enumerate(ORDER):
+    for i, (m, started, now) in enumerate(ORDER):
         transfer(m).wait_recv()
+        leaving += [(other, now) for other in started]
+        while leaving and now - leaving[0][1] > 20.0:
+            transfer(leaving.pop(0)[0]).wait_send()
         for other in started:
             transfer(other).start()
         if i == ids_left:
@@ -358,7 +364,7 @@
         factor[s] = (jnp.where(eye, scale, 0.0) - 0.5 * square).astype(jnp.bfloat16)
         return carry
 
-    lax.fori_loop(0, SLOTS, one_slot, 0, unroll=4)
+    lax.fori_loop(0, SLOTS, one_slot, 0, unroll=6)
 
     for k in range(1, NY):
         sum_transfer("y", k).wait_recv()
@@ -367,7 +373,7 @@
         total = total + y_sums[k]
     trace[0, 0] = jnp.max(total) * (1.0 / (NB * BS))
 
-    for m in SIZE:
+    for m, _ in leaving:
         transfer(m).wait_send()
     for axis, extent in (("x", NX), ("y", NY)):
         for k in range(1, extent):

time: 96.9 us -> 96.5 us (level)
  the two profiles are of different devices: /device:TPU:28 before, /device:TPU:30 now
where the time goes in v3:
time: 96.5 us; the launch traced here: 96.3 us
  Pallas kernels  92.1 us (95%)
  between operations  2.39 us (2%)
  local copies, waits for them, and re-layouts  1.77 us (2%)
    pallas_call x1, Pallas kernels, shards(): pl.pallas_call(kernel, out_shape=(jax.ShapeDtypeStruct((SLOTS, BS, BS), j...  92.1 us

profile of v3, /device:TPU:30, one launch (start us, length us, event | category | flops | bytes accessed | tf_op | source)
XLA Modules:
  0.0 96.3 jit_solution(3659465512804732009)
XLA Ops:
  0.6 92.1 %shard_map.50 = (bf16[12,128,128]{2,1,0:T(8,128)(2,1)}, f32[1,1]{1,0:T(1,128)}) custom-call(bf16[1536,128]{1,0:T(8,128)(2,1)} %bitcast.5, s32[12]{0:T(128)} %bitcast.7, s32[12]{0:T(128)} %bitcast.8), custom_call_target="tpu_custom_call" | custom-call | tf_op jit(solution)/shard_map/pallas_call | solution.py:386
  92.8 1.8 %copy.7 = bf16[1,1,12,128,128]{4,3,2,1,0:T(8,128)(2,1)} copy(bf16[1,1,12,128,128]{4,3,2,1,0:T(8,128)(2,1)} %bitcast.6) | data formatting | bytes 786432
